TPU v7x, 128 devices: a whole 4x4x4 slice. The times are simulated.
128 devices in a mesh: row: 8 (over x, core), col: 16 (over y, z).
Axes of the slice: x: 4, y: 4, z: 4, core: 2. Of those that a mesh axis runs over, the one named last changes fastest.
Arguments:
- filtered: float32 [32768, 2048], P(('row', 'col')), as said below
- hamiltonian_applied: float32 [32768, 2048], P(('row', 'col')), as said below
- rotation: float32 [2048, 2048], replicated, may hold values from -0.125 to 0.125
Outputs:
- intersection: float32 [2048, 2048], P('row', 'col')
- projected: float32 [2048, 2048], P('row', 'col')
- rotated: float32 [32768, 2048], P(('row', 'col'))
Inputs may be any that keep to these rules, and one draw needn't show every extreme that they name: `filtered`: finite real values. `hamiltonian_applied`: finite real values.
All inputs are finite; a program needn't handle non-finite values.
Results may differ from a plain program's by a relative error of at most 0.00005.
Values sent between devices are 32-bit elements; how exact they have to be, the bound alone decides.
A program may use at most 192 MiB of HBM per device.

v0:
```python
import jax
import jax.numpy as jnp
from jax import lax
from jax.sharding import PartitionSpec as P


def inner_rows(first, second):
    return jnp.einsum(
        "gi,gj->ij",
        first,
        second,
        precision=lax.Precision.HIGHEST,
        preferred_element_type=jnp.float32,
    )


def product(first, second):
    return jnp.dot(
        first, second, precision=lax.Precision.HIGHEST, preferred_element_type=jnp.float32
    )


def local(filtered, hamiltonian_applied, rotation):
    cells = filtered.shape[0]
    col_count = lax.axis_size("col")
    row_count = lax.axis_size("row")
    scale = 1.0 / (cells * col_count * row_count)
    psi_band, ham_band = (
        lax.all_to_all(filtered, "col", split_axis=1, concat_axis=0, tiled=True),
        lax.all_to_all(hamiltonian_applied, "col", split_axis=1, concat_axis=0, tiled=True),
    )
    piece = lax.all_gather(psi_band, "col", axis=1, tiled=True)
    over_term = inner_rows(piece, psi_band) * scale
    proj_term = inner_rows(piece, ham_band) * scale
    over_term, proj_term = (over_term, proj_term)
    intersection, projected = (
        lax.psum_scatter(over_term, "row", scatter_dimension=0, tiled=True),
        lax.psum_scatter(proj_term, "row", scatter_dimension=0, tiled=True),
    )
    rotated = product(filtered, rotation)
    return (intersection, projected, rotated)


def solution(mesh):
    return jax.shard_map(
        local,
        mesh=mesh,
        in_specs=(P(("row", "col"), None), P(("row", "col"), None), P()),
        out_specs=(P("row", "col"), P("row", "col"), P(("row", "col"), None)),
        check_vma=False,
    )
```

profile of v0, /device:TPU:0, one launch (start us, length us, event | category | flops | bytes accessed | tf_op | source)
XLA Modules:
  0.0 426.3 jit_solution(1615125823483766629)
XLA Ops:
  7.2 0.0 all-gather.2.cloned.1.call-start
  7.2 2.9 copy.6
  10.1 36.4 %all_to_all.38 = f32[256,16,128]{0,2,1:T(8,128)S(1)} all-to-all(f32[256,16,128]{0,2,1:T(8,128)} %bitcast.17), channel_id=1, replica_groups=mesh['row'=8,'col'=16] {'col'}, dimensions={1} | all-to-all | bytes 4194304 | tf_op jit(solution)/shard_map/all_to_all | solution.py:29
  46.5 1.8 copy.7
  48.3 0.0 copy-start.2
  48.3 0.0 all-gather.2.cloned.1.call-update
  48.3 1.6 copy-done.2
  49.9 1.9 copy.8
  51.7 0.0 copy-start
  51.8 4.6 %all-to-all-start.1 = ((f32[256,16,128]{0,2,1:T(8,128)}), f32[256,16,128]{0,2,1:T(8,128)}, u32[]{:S(2)}, u32[]{:S(2)}) async-start(f32[256,16,128]{0,2,1:T(8,128)} %bitcast.15), calls=%async_computation.2 | async-start | bytes 4194304 | tf_op jit(solution)/shard_map/all_to_all | solution.py:30
  56.3 0.0 reduce-scatter.3.cloned.1.call-start
  56.4 215.1 %all-gather.2.cloned.1.call-done = f32[4096,2048]{1,0:T(8,128)} async-done(((f32[4096,128]{1,0:T(8,128)}), f32[4096,2048]{1,0:T(8,128)}) %all-gather.2.cloned.1.call-update) | async-done | bytes 33554448 | tf_op jit(solution)/shard_map/all_gather | solution.py:32
  271.5 0.0 copy-done
  271.5 56.6 %convolution_multiply_fusion.1 = f32[2048,128]{1,0:T(8,128)} fusion(f32[4096,2048]{1,0:T(8,128)} %all-gather.2.cloned.1.call-done, f32[4096,128]{1,0:T(8,128)S(1)} %bitcast.13), kind=kOutput, calls=%fused_computation.1 | convolution fusion | flops 12885164032 | bytes 36700160 | tf_op jit(solution)/shard_map/gi,gj->ij/dot_general | solution.py:8
  328.1 0.0 reduce-scatter.3.cloned.1.call-update
  328.1 0.0 reduce-scatter.5.cloned.1.call-start
  328.2 0.0 all-to-all-done.1
  328.2 2.9 copy.9
  331.1 0.0 copy-start.1
  331.1 57.4 %convolution_multiply_fusion = f32[2048,128]{1,0:T(8,128)} fusion(f32[4096,2048]{1,0:T(8,128)} %all-gather.2.cloned.1.call-done, f32[4096,128]{1,0:T(8,128)} %bitcast.14), kind=kOutput, calls=%fused_computation | convolution fusion | flops 12885164032 | bytes 36700160 | tf_op jit(solution)/shard_map/gi,gj->ij/dot_general | solution.py:8
  388.5 0.0 reduce-scatter.5.cloned.1.call-update
  388.5 0.0 copy-done.1
  388.5 17.8 %fusion = f32[256,2048]{1,0:T(8,128)} fusion(f32[256,2048]{1,0:T(8,128)S(1)} %copy-done.1, f32[2048,2048]{1,0:T(8,128)} %param.5), kind=kOutput, calls=%fused_computation.2 | convolution fusion | flops 12884901888 | bytes 20971520 | tf_op jit(solution)/shard_map/dot_general | solution.py:18
  406.3 0.0 reduce-scatter.3.cloned.1.call-done
  406.3 13.4 %reduce-scatter.5.cloned.1.call-done = f32[256,128]{1,0:T(8,128)} async-done(((f32[2048,128]{1,0:T(8,128)}), f32[256,128]{1,0:T(8,128)}) %reduce-scatter.5.cloned.1.call-update) | async-done | bytes 131088 | tf_op jit(solution)/shard_map/reduce_scatter | solution.py:38
Async XLA Ops:
  7.2 264.3 %all-gather.2.cloned.1.call-start = ((), (), s32[]{:S(2)}) async-start(), calls=%async_computation.4 | async-start | bytes 35651584 | tf_op jit(solution)/shard_map/all_gather | solution.py:32
  48.3 1.6 copy-start.2
  51.7 219.7 %copy-start = (f32[16,256,128]{2,1,0:T(8,128)S(1)}, f32[16,256,128]{2,1,0:T(8,128)}, u32[]{:S(2)}) copy-start(f32[16,256,128]{2,1,0:T(8,128)} %copy.7) | copy-start | bytes 6291460
  51.8 276.4 %all-to-all-start.1 = ((f32[256,16,128]{0,2,1:T(8,128)}), f32[256,16,128]{0,2,1:T(8,128)}, u32[]{:S(2)}, u32[]{:S(2)}) async-start(f32[256,16,128]{0,2,1:T(8,128)} %bitcast.15), calls=%async_computation.2 | async-start | bytes 4194304 | tf_op jit(solution)/shard_map/all_to_all | solution.py:30
  56.3 350.0 %reduce-scatter.3.cloned.1.call-start = ((), (), s32[]{:S(2)}) async-start(), calls=%async_computation.5 | async-start | bytes 1179648 | tf_op jit(solution)/shard_map/reduce_scatter | solution.py:37
  328.1 91.6 %reduce-scatter.5.cloned.1.call-start = ((), (), s32[]{:S(2)}) async-start(), calls=%async_computation.6 | async-start | bytes 1179648 | tf_op jit(solution)/shard_map/reduce_scatter | solution.py:38
  331.1 57.4 %copy-start.1 = (f32[256,2048]{1,0:T(8,128)S(1)}, f32[256,2048]{1,0:T(8,128)}, u32[]{:S(2)}) copy-start(f32[256,2048]{1,0:T(8,128)} %param.3) | copy-start | bytes 6291460
Sparse Core Ops, SparseCore 0:
  48.4 223.0 all-gather.1
  328.3 31.0 reduce-scatter.2
  388.6 31.0 reduce-scatter.4
where the time goes:
time: 427 us; the launch traced here: 426 us
  waiting for transfers between devices  229 us (54%)
  matrix products  132 us (31%)
  blocking collectives  36.4 us (9%)
  between operations  13.8 us (3%)
  local copies, waits for them, and re-layouts  11 us (3%)
  starting transfers between devices  4.7 us (1%)
    all_gather x1, waiting for transfers between devices, local(): piece = lax.all_gather(psi_band, 'col', axis=1, tiled=True)  215 us
    dot_general x2, matrix products, inner_rows(): jnp.einsum('gi,gj->ij', first, second, precision=lax.Precision.HIGHEST, p...  114 us
    all_to_all x1, blocking collectives, local(): lax.all_to_all(filtered, 'col', split_axis=1, concat_axis=0, tiled=True)  36.4 us
    dot_general x1, matrix products, product(): jnp.dot(first, second, precision=lax.Precision.HIGHEST, preferred_element...  17.8 us
    reduce_scatter x1, waiting for transfers between devices, local(): lax.psum_scatter(proj_term, 'row', scatter_dimension=0, tiled=True)  13.4 us
  transfers between devices with their start and end apart: 4, of which 2 were waited for; matrix products, arithmetic and copies ran while one was open for 32% of the time, Pallas kernels for 0%

commit v1 on v0

--- a/solution.py
+++ b/solution.py
@@ -29,7 +29,10 @@
         lax.all_to_all(filtered, "col", split_axis=1, concat_axis=0, tiled=True),
         lax.all_to_all(hamiltonian_applied, "col", split_axis=1, concat_axis=0, tiled=True),
     )
-    piece = lax.all_gather(psi_band, "col", axis=1, tiled=True)
+    size = lax.axis_size("col")
+    pieces = jnp.stack([psi_band for _ in range(size)])
+    pieces = lax.all_to_all(pieces, "col", split_axis=0, concat_axis=0)
+    piece = jnp.concatenate(pieces, axis=1)
     over_term = inner_rows(piece, psi_band) * scale
     proj_term = inner_rows(piece, ham_band) * scale
     over_term, proj_term = (over_term, proj_term)

time: 427 us -> 795 us (1.86)
  waiting for transfers between devices: 229 us -> 623 us
  matrix products: 132 us -> 79.6 us
  starting transfers between devices: 4.7 us -> 17.5 us
  local copies, waits for them, and re-layouts: 11 us -> 23.6 us
    all_to_all x0 -> x1, waiting for transfers between devices: none -> 607 us  [local(): pieces = lax.all_to_all(pieces, 'col', split_axis=0, concat_axis=0)]
    all_gather x1 -> x0, waiting for transfers between devices: 215 us -> none  [local(): piece = lax.all_gather(psi_band, 'col', axis=1, tiled=True)]
    dot_general x2, matrix products: 114 us -> 61.9 us  [inner_rows(): jnp.einsum('gi,gj->ij', first, second, precision=lax.Precision.HIGHEST, p...]
    another operation x0 -> x2, local copies, waits for them, and re-layouts: none -> 14 us  [local(): pieces = jnp.stack([psi_band for _ in range(size)])]
  transfers between devices with their start and end apart: 4 -> 4, of which waited for: 2 -> 2; matrix products, arithmetic and copies ran while one was open for 32% -> 11% of each run, Pallas kernels for 0% -> 0%
where the time goes in v1:
time: 795 us; the launch traced here: 794 us
  waiting for transfers between devices  623 us (78%)
  matrix products  79.6 us (10%)
  blocking collectives  36.3 us (5%)
  local copies, waits for them, and re-layouts  23.6 us (3%)
  starting transfers between devices  17.5 us (2%)
  between operations  14.1 us (2%)
    all_to_all x1, waiting for transfers between devices, local(): pieces = lax.all_to_all(pieces, 'col', split_axis=0, concat_axis=0)  607 us
    dot_general x2, matrix products, inner_rows(): jnp.einsum('gi,gj->ij', first, second, precision=lax.Precision.HIGHEST, p...  61.9 us
    all_to_all x1, blocking collectives, local(): lax.all_to_all(filtered, 'col', split_axis=1, concat_axis=0, tiled=True)  36.3 us
    dot_general x1, matrix products, product(): jnp.dot(first, second, precision=lax.Precision.HIGHEST, preferred_element...  17.8 us
  transfers between devices with their start and end apart: 4, of which 2 were waited for; matrix products, arithmetic and copies ran while one was open for 11% of the time, Pallas kernels for 0%

profile of v1, /device:TPU:0, one launch (start us, length us, event | category | flops | bytes accessed | tf_op | source)
XLA Modules:
  0.0 794.3 jit_solution(493579519644329692)
XLA Ops:
  7.2 1.9 copy.7
  9.1 36.3 %all_to_all.40 = f32[256,16,128]{0,2,1:T(8,128)} all-to-all(f32[256,16,128]{0,2,1:T(8,128)S(1)} %bitcast.20), channel_id=1, replica_groups=mesh['row'=8,'col'=16] {'col'}, dimensions={1} | all-to-all | bytes 4194304 | tf_op jit(solution)/shard_map/all_to_all | solution.py:29
  45.4 1.9 copy.8
  47.3 1.8 copy.9
  49.1 12.2 %stack.5 = f32[16,4096,128]{1,2,0:T(8,128)} broadcast(f32[4096,128]{0,1:T(8,128)} %copy.9), dimensions={1,2} | broadcast | bytes 35651584 | tf_op jit(solution)/shard_map/stack | solution.py:33
  61.3 5.9 all-to-all-start.1
  67.2 2.9 copy.10
  70.1 607.5 %all-to-all-done.1 = f32[16,4096,128]{1,2,0:T(8,128)} async-done(((f32[16,4096,128]{1,2,0:T(8,128)}), f32[16,4096,128]{1,2,0:T(8,128)}, u32[]{:S(2)}, u32[]{:S(2)}) %all-to-all-start.1) | async-done | bytes 33554464 | tf_op jit(solution)/shard_map/all_to_all | solution.py:34
  677.6 11.3 %all-to-all-start.2 = ((f32[256,16,128]{0,2,1:T(8,128)}), f32[256,16,128]{0,2,1:T(8,128)}, u32[]{:S(2)}, u32[]{:S(2)}) async-start(f32[256,16,128]{0,2,1:T(8,128)} %bitcast.18), calls=%async_computation.3 | async-start | bytes 4194304 | tf_op jit(solution)/shard_map/all_to_all | solution.py:30
  688.9 0.0 reduce-scatter.3.cloned.1.call-start
  688.9 30.8 %convolution_multiply_fusion.1 = f32[2048,128]{1,0:T(8,128)} fusion(f32[4096,2048]{0,1:T(8,128)} %bitcast.4, f32[4096,128]{1,0:T(8,128)S(1)} %bitcast.16), kind=kOutput, calls=%fused_computation.1 | convolution fusion | flops 12885164032 | bytes 36700160 | tf_op jit(solution)/shard_map/gi,gj->ij/dot_general | solution.py:8
  719.7 0.0 reduce-scatter.3.cloned.1.call-update
  719.7 0.2 reduce-scatter.5.cloned.1.call-start
  719.9 0.0 all-to-all-done.2
  720.0 2.9 copy.11
  722.8 0.0 copy-start
  722.8 31.1 %convolution_multiply_fusion = f32[2048,128]{1,0:T(8,128)} fusion(f32[4096,2048]{0,1:T(8,128)} %bitcast.4, f32[4096,128]{1,0:T(8,128)} %bitcast.17), kind=kOutput, calls=%fused_computation | convolution fusion | flops 12885164032 | bytes 36700160 | tf_op jit(solution)/shard_map/gi,gj->ij/dot_general | solution.py:8
  753.9 0.0 reduce-scatter.5.cloned.1.call-update
  754.0 0.0 copy-done
  754.0 17.8 %fusion = f32[256,2048]{1,0:T(8,128)} fusion(f32[256,2048]{1,0:T(8,128)S(1)} %copy-done, f32[2048,2048]{1,0:T(8,128)} %param.5), kind=kOutput, calls=%fused_computation.2 | convolution fusion | flops 12884901888 | bytes 20971520 | tf_op jit(solution)/shard_map/dot_general | solution.py:18
  771.7 0.0 reduce-scatter.3.cloned.1.call-done
  771.7 15.7 %reduce-scatter.5.cloned.1.call-done = f32[256,128]{1,0:T(8,128)} async-done(((f32[2048,128]{1,0:T(8,128)}), f32[256,128]{1,0:T(8,128)}) %reduce-scatter.5.cloned.1.call-update) | async-done | bytes 131088 | tf_op jit(solution)/shard_map/reduce_scatter | solution.py:41
Async XLA Ops:
  61.3 616.3 %all-to-all-start.1 = ((f32[16,4096,128]{1,2,0:T(8,128)}), f32[16,4096,128]{1,2,0:T(8,128)}, u32[]{:S(2)}, u32[]{:S(2)}) async-start(f32[16,4096,128]{1,2,0:T(8,128)} %stack.5), calls=%async_computation.1 | async-start | bytes 67108864 | tf_op jit(solution)/shard_map/all_to_all | solution.py:34
  677.6 42.4 %all-to-all-start.2 = ((f32[256,16,128]{0,2,1:T(8,128)}), f32[256,16,128]{0,2,1:T(8,128)}, u32[]{:S(2)}, u32[]{:S(2)}) async-start(f32[256,16,128]{0,2,1:T(8,128)} %bitcast.18), calls=%async_computation.3 | async-start | bytes 4194304 | tf_op jit(solution)/shard_map/all_to_all | solution.py:30
  688.9 82.9 %reduce-scatter.3.cloned.1.call-start = ((), (), s32[]{:S(2)}) async-start(), calls=%async_computation.5 | async-start | bytes 1179648 | tf_op jit(solution)/shard_map/reduce_scatter | solution.py:40
  719.7 67.7 %reduce-scatter.5.cloned.1.call-start = ((), (), s32[]{:S(2)}) async-start(), calls=%async_computation.6 | async-start | bytes 1179648 | tf_op jit(solution)/shard_map/reduce_scatter | solution.py:41
  722.8 31.1 %copy-start = (f32[256,2048]{1,0:T(8,128)S(1)}, f32[256,2048]{1,0:T(8,128)}, u32[]{:S(2)}) copy-start(f32[256,2048]{1,0:T(8,128)} %param.3) | copy-start | bytes 6291460
Sparse Core Ops, SparseCore 0:
  719.8 33.3 reduce-scatter.2
  756.2 31.2 reduce-scatter.4
